TPU v7x, 32 devices: a whole 2x2x4 slice. The times are simulated.
32 devices in a mesh: grp: 8 (over z, core), dev: 4 (over y, x).
Axes of the slice: x: 2, y: 2, z: 4, core: 2. Of those that a mesh axis runs over, the one named last changes fastest.
Arguments:
- orbitals: bfloat16 [64, 256, 1024], P(('grp', 'dev')), may hold values from -6 to 6
- dens_tiles: bfloat16 [1024, 128, 128], P(('grp', 'dev')), may hold values from -0.005859375 to 0.005859375
- point_coords: float32 [3, 16384], P(None, ('grp', 'dev')), may hold values from 0 to 64
- point_weights: float32 [16384], P(('grp', 'dev')), may hold values from 0.005 to 0.05
- batch_blocks: int32 [64, 8], P(('grp', 'dev')), may hold values from 0 to 8, all different within a row
- tile_owner: int32 [2592, 1], P(('grp', 'dev')), may hold values from 0 to 3; in each aligned block of 81 rows (0 to 80, 81 to 161, ...) at most 31 rows name the same one
- tile_slot: int32 [2592], P(('grp', 'dev')), may hold values from 0 to 31
- batch_atoms: int32 [64, 4], P(('grp', 'dev')), may hold values from 0 to 3, all different within a row
- batch_weights: int32 [64, 4], P(('grp', 'dev')), may hold values from 1 to 8
- atom_grid_index: int32 [3, 32], P(None, 'grp'), may hold values from 0 to 63
Outputs:
- density: float32 [16384], P(('grp', 'dev'))
- potential: float32 [16384], P(('grp', 'dev'))
- ham_tiles: bfloat16 [1024, 128, 128], P(('grp', 'dev'))
Inputs may be any that keep to these rules, and one draw needn't show every extreme that they name: `tile_owner`: in each aligned block of 81 rows (the listed tiles of one device) no owner is named by more than 31 rows, a bound that some block reaches. `batch_blocks`: the 8 blocks of a batch are distinct. `batch_atoms`: the 4 atoms of a batch are distinct.
All inputs are finite; a program needn't handle non-finite values.
Results may differ from a plain program's by a relative error of at most 0.0056.
Values may be sent and summed in bfloat16 or wider, within the bound.
A program may use at most 64 MiB of HBM per device.

v0:
```python
import math

import jax
import jax.numpy as jnp
from jax import lax
from jax.sharding import PartitionSpec as P

TB = 128
BB = 8
UB = 9
PTS = 256
BAT_DEV = 2
KM = 512
TILE_DEV = 32
GRIDN = 64


TOP_PRECISION = lax.Precision.HIGHEST


def wave_table(count):
    mode_ids = jnp.arange(count // 2, dtype=jnp.int32)
    return jnp.stack([mode_ids % 8, mode_ids // 8 % 8, mode_ids // 64]).astype(jnp.float32)


def kernel_gains(count):
    wave_vecs = wave_table(count)
    squared = jnp.sum(wave_vecs * wave_vecs, axis=0)
    near_gain = 0.1 / (1.0 + 0.1 * squared)
    far_gain = 0.03 / (1.0 + 0.1 * squared)
    return (jnp.concatenate([near_gain, near_gain]), jnp.concatenate([far_gain, far_gain]))


def local_basis(coords, centre_points, wave_vecs, grid_extent):
    displace = coords[:, :, None, :] - centre_points[:, :, :, None]
    phases = jnp.einsum("cbnp,cm->bnpm", displace, wave_vecs, precision=TOP_PRECISION) * (
        2.0 * math.pi / grid_extent
    )
    envelope = jnp.exp(-2.0 * jnp.sum(displace * displace, axis=0) / (grid_extent * grid_extent))
    return envelope[..., None] * jnp.concatenate([jnp.cos(phases), jnp.sin(phases)], axis=-1)


def wave_values(coords, wave_vecs, grid_extent):
    phases = jnp.einsum("cbp,cm->bpm", coords, wave_vecs, precision=TOP_PRECISION) * (
        2.0 * math.pi / grid_extent
    )
    return jnp.concatenate([jnp.cos(phases), jnp.sin(phases)], axis=-1)


def on_device(
    orbitals,
    dens_tiles,
    point_coords,
    point_weights,
    batch_blocks,
    tile_owner,
    tile_slot,
    batch_atoms,
    batch_weights,
    atom_grid_index,
):
    owner_count = lax.axis_size("dev")
    listed = tile_slot.shape[0]
    capacity = max(2, (listed + owner_count - 1) // owner_count * 3 // 2)
    owner_ids = tile_owner[:, 0]
    owner_hot = (owner_ids[:, None] == jnp.arange(owner_count, dtype=jnp.int32)[None, :]).astype(
        jnp.int32
    )
    bucket_rank = jnp.sum(jnp.cumsum(owner_hot, axis=0) * owner_hot, axis=1) - 1
    send_place = owner_ids * capacity + bucket_rank
    outgoing = jnp.full((owner_count * capacity,), -1, jnp.int32).at[send_place].set(tile_slot)
    requested_tiles = lax.all_to_all(outgoing, "dev", split_axis=0, concat_axis=0, tiled=True)
    wanted_index = owner_ids * TILE_DEV + tile_slot
    portion = lax.all_gather(dens_tiles, "dev", axis=0, tiled=True)
    inside = (wanted_index >= 0) & (wanted_index < portion.shape[0])
    picked = portion[jnp.clip(wanted_index, 0, portion.shape[0] - 1)]
    local_tiles = jnp.where(
        inside[:, None, None], picked, jnp.zeros((listed, TB, TB), jnp.bfloat16)
    )
    wave_vecs = wave_table(KM)
    near_gain, far_gain = kernel_gains(KM)
    coords = point_coords.reshape(3, BAT_DEV, PTS)
    weights = point_weights.reshape(BAT_DEV, PTS)
    atom_location = atom_grid_index.astype(jnp.float32)
    atom_onehot_rows = (
        batch_atoms[:, :, None]
        == jnp.arange(atom_grid_index.shape[1], dtype=jnp.int32)[None, None, :]
    ).astype(jnp.float32)
    centre_points = jnp.einsum(
        "dxp,qp->qdx", atom_onehot_rows, atom_location, precision=TOP_PRECISION
    )
    ebasis = local_basis(coords, centre_points, wave_vecs, GRIDN)
    raw_weight = batch_weights.astype(jnp.float32)
    partition = raw_weight / jnp.sum(raw_weight, axis=1, keepdims=True)

    def density_step(unused, inputs):
        orbital, chosen = inputs
        block_index = chosen[:, None] * UB + chosen[None, :]
        dens_block = local_tiles[block_index].transpose(0, 2, 1, 3).reshape(BB * TB, BB * TB)
        product = jnp.dot(orbital, dens_block, preferred_element_type=jnp.float32)
        return (unused, jnp.sum(product * orbital.astype(jnp.float32), axis=1))

    unused, density = lax.scan(density_step, jnp.zeros((), jnp.float32), (orbitals, batch_blocks))
    coeffs = partition[:, :, None] * jnp.einsum(
        "bp,bnpk->bnk", weights * density, ebasis, precision=TOP_PRECISION
    )
    moments_dev = jnp.einsum("bna,bnk->ak", atom_onehot_rows, coeffs, precision=TOP_PRECISION)
    atom_trig = wave_values(atom_location[:, None, :], wave_vecs, GRIDN)[0]
    moments_grp = lax.psum(moments_dev, "dev")
    structure = lax.psum(jnp.dot(moments_grp[:, 0], atom_trig, precision=TOP_PRECISION), "grp")
    coef_near = near_gain[None, :] * moments_grp
    chosen_coef = jnp.einsum("bna,ak->bnk", atom_onehot_rows, coef_near, precision=TOP_PRECISION)
    near_val = jnp.sum(
        partition[:, :, None]
        * jnp.einsum("bnpk,bnk->bnp", ebasis, chosen_coef, precision=TOP_PRECISION),
        axis=1,
    )
    far_val = jnp.einsum(
        "bpk,k->bp",
        wave_values(coords, wave_vecs, GRIDN),
        far_gain * structure,
        precision=TOP_PRECISION,
    )
    potential = near_val + far_val

    def hamilton_step(ham_local, inputs):
        orbital, chosen, scaled_pot = inputs
        scaled_orb = (scaled_pot[:, None] * orbital.astype(jnp.float32)).astype(jnp.bfloat16)
        ham_batch = lax.dot_general(
            orbital, scaled_orb, (((0,), (0,)), ((), ())), preferred_element_type=jnp.float32
        )
        pieces = ham_batch.reshape(BB, TB, BB, TB).transpose(0, 2, 1, 3).reshape(BB * BB, TB, TB)
        block_index = (chosen[:, None] * UB + chosen[None, :]).reshape(-1)
        return (ham_local.at[block_index].add(pieces), None)

    ham_local, unused_out = lax.scan(
        hamilton_step,
        jnp.zeros((listed, TB, TB), jnp.float32),
        (orbitals, batch_blocks, weights * potential),
    )
    ham_out = (
        jnp.zeros((owner_count * capacity, TB, TB), jnp.bfloat16)
        .at[send_place]
        .set(ham_local.astype(jnp.bfloat16))
    )
    returned = lax.all_to_all(ham_out, "dev", split_axis=0, concat_axis=0, tiled=True)
    slot_onehot_rows = (
        jnp.arange(TILE_DEV, dtype=jnp.int32)[:, None] == requested_tiles[None, :]
    ).astype(jnp.bfloat16)
    ham_tiles = jnp.dot(
        slot_onehot_rows,
        returned.reshape(owner_count * capacity, TB * TB),
        preferred_element_type=jnp.float32,
    )
    return (
        density.reshape(-1),
        potential.reshape(-1),
        ham_tiles.reshape(TILE_DEV, TB, TB).astype(jnp.bfloat16),
    )


def solution(mesh):
    in_specs = (
        P(("grp", "dev"), None, None),
        P(("grp", "dev"), None, None),
        P(None, ("grp", "dev")),
        P(("grp", "dev")),
        P(("grp", "dev"), None),
        P(("grp", "dev"), None),
        P(("grp", "dev")),
        P(("grp", "dev"), None),
        P(("grp", "dev"), None),
        P(None, "grp"),
    )
    out_specs = (P(("grp", "dev")), P(("grp", "dev")), P(("grp", "dev"), None, None))
    return jax.shard_map(
        on_device, mesh=mesh, in_specs=in_specs, out_specs=out_specs, check_vma=False
    )
```

profile of v0, /device:TPU:0, one launch (start us, length us, event | category | flops | bytes accessed | tf_op | source)
XLA Modules:
  0.0 240.3 jit_solution(1838354967024481996)
XLA Ops:
  11.9 5.2 %all-to-all-start = ((s32[4,31,1]{1,2,0:T(1,128)}), s32[4,31,1]{1,2,0:T(1,128)S(1)}, u32[]{:S(2)}, u32[]{:S(2)}) async-start(s32[4,31,1]{1,2,0:T(1,128)} %bitcast.44), calls=%async_computation | async-start | bytes 4096 | tf_op jit(solution)/shard_map/all_to_all | solution.py:72
  23.6 4.2 %cosine_bitcast_fusion = (f32[2,256,256]{1,2,0:T(8,128)}, f32[2,256,256]{1,2,0:T(8,128)}) fusion(f32[3,2,256]{2,0,1:T(4,128)} %bitcast.173, s32[1,256]{1,0:T(1,128)S(1)} %get-tuple-element.125, s32[1,256]{1,0:T(1,128)S(1)} %get-tuple-element.126, s32[1,256]{1,0:T(1,128)S(1)} %and_select_fusion.3), kind=kOutput, calls=%fused_computation.47 | convolution fusion | flops 4851968 | bytes 1057792 | tf_op jit(solution)/shard_map/cbp,cm->bpm/dot_general | solution.py:44
  27.8 12.3 %multiply_cosine_fusion = (f32[2,4,256,256]{2,3,1,0:T(8,128)}, f32[2,4,256,256]{2,3,1,0:T(8,128)}) fusion(s32[1,256]{1,0:T(1,128)S(1)} %get-tuple-element.125, s32[1,256]{1,0:T(1,128)S(1)} %get-tuple-element.126, s32[1,256]{1,0:T(1,128)S(1)} %and_select_fusion.3, f32[3,2,4]{0,2,1:T(4,128)S(1)} %copy.38, f32[3,2,256]{2,0,1:T(4,128)} %bitcast.174), kind=kOutput, calls=%fused_computation.35 | convolution fusion | flops 19407104 | bytes 4203616 | tf_op jit(solution)/shard_map/cbnp,cm->bnpm/dot_general | solution.py:36
  40.0 25.2 %all-gather.2.cloned.1.call-done = bf16[128,128,128]{2,1,0:T(8,128)(2,1)} async-done(((bf16[32,128,128]{2,1,0:T(8,128)(2,1)}), bf16[128,128,128]{2,1,0:T(8,128)(2,1)}) %all-gather.2.cloned.1.call-update) | async-done | bytes 4194320 | tf_op jit(solution)/shard_map/all_gather | solution.py:74
  65.3 3.2 %gather_fusion.1 = bf16[81,128,128]{2,1,0:T(8,128)(2,1)S(1)} fusion(bf16[128,128,128]{2,1,0:T(8,128)(2,1)} %all-gather.2.cloned.1.call-done, s32[1024]{0:T(1024)S(1)} %pad_clamp_fusion.1), kind=kCustom, calls=%fused_computation.1 | custom fusion | bytes 5308740 | tf_op jit(solution)/shard_map/gather | solution.py:76
  70.3 10.3 %while.20 = (s32[]{:T(128)}, f32[2,256]{1,0:T(2,128)S(1)}, bf16[2,256,1024]{2,1,0:T(8,128)(2,1)}, s32[2,8]{1,0:T(2,128)S(1)}, bf16[81,128,128]{2,1,0:T(8,128)(2,1)}, /*index=5*/s32[]{:T(128)}, s32[]{:T(128)}) while((s32[]{:T(128)}, f32[2,256]{1,0:T(2,128)S(1)}, bf16[2,256,1024]{2,1,0:T(8,128)(2,1)}, s32[2,8]{1,0:T(2,128)S(1)}, ...), condition=%wide.region_2.3_spmd, body=%wide.region_0.2_spmd.sunk | while | flops 537658368 | bytes 15738385 | solution.py:103
  70.5 2.7 %gather_fusion = bf16[64,128,128]{2,1,0:T(8,128)(2,1)S(1)} fusion(bf16[81,128,128]{2,1,0:T(8,128)(2,1)} %get-tuple-element.215, s32[1024]{0:T(1024)S(1)} %pad_clamp_fusion.3), kind=kCustom, calls=%fused_computation.clone.1 | custom fusion | bytes 4194560 | tf_op jit(solution)/shard_map/while/body/eval_jaxpr/gather | solution.py:99
  80.6 5.9 %fusion.17 = f32[2,1,4,512]{3,1,2,0:T(1,128)S(1)} fusion(f32[2,4,256,256]{2,3,1,0:T(8,128)} %get-tuple-element.116, f32[2,4,256,256]{2,3,1,0:T(8,128)} %get-tuple-element.115, f32[2,4,256]{2,1,0:T(4,128)S(1)} %multiply_exponential_fusion, f32[2,256,1,1]{1,0,2,3:T(2,128)S(1)} %multiply_bitcast_fusion), kind=kOutput, calls=%fused_computation.30 | convolution fusion | flops 14680064 | bytes 4220928 | tf_op jit(solution)/shard_map/bp,bnpk->bnk/dot_general | solution.py:104
  86.8 9.2 %psum.14 = f32[4,512]{1,0:T(4,128)S(1)} all-reduce(f32[4,512]{1,0:T(4,128)S(1)} %convolution_bitcast_fusion.1), channel_id=1, replica_groups=mesh['grp'=8,'dev'=4] {'dev'}, use_global_device_ids=true, to_apply=%region_6.7 | all-reduce | flops 2048 | bytes 16384 | tf_op jit(solution)/shard_map/psum | solution.py:109
  96.2 14.3 %psum.15 = f32[512]{0:T(512)S(1)} all-reduce(f32[512]{0:T(512)S(1)} %bitcast.182), channel_id=1, replica_groups=mesh['grp'=8,'dev'=4] {'grp'}, use_global_device_ids=true, to_apply=%region_8.9 | all-reduce | flops 512 | bytes 4096 | tf_op jit(solution)/shard_map/psum | solution.py:110
  110.8 4.0 %fusion.16 = f32[2,4,1,256]{3,2,1,0:T(1,128)S(1)} fusion(f32[2,4,256,256]{2,3,1,0:T(8,128)} %get-tuple-element.116, f32[2,4,256,256]{2,3,1,0:T(8,128)S(1)} %copy-done, f32[2,4,256]{2,1,0:T(4,128)S(1)} %multiply_exponential_fusion, f32[2,4,512,1]{2,1,0,3:T(4,128)S(1)} %convolution_bitcast_fusion), kind=kOutput, calls=%fused_computation.29 | convolution fusion | flops 14680064 | bytes 4227072 | tf_op jit(solution)/shard_map/bnpk,bnk->bnp/dot_general | solution.py:115
  115.5 3.0 %broadcast_in_dim.41 = f32[81,128,128]{2,1,0:T(8,128)} broadcast(f32[]{:T(128)} %constant.113.clone.1), dimensions={} | broadcast | bytes 5308420 | tf_op jit(solution)/shard_map/broadcast_in_dim | solution.py:138
  118.5 34.0 %while.21 = (s32[]{:T(128)}, f32[81,128,128]{2,1,0:T(8,128)}, s32[2,8]{1,0:T(2,128)S(1)}, bf16[2,256,1024]{2,1,0:T(8,128)(2,1)S(1)}, f32[2,256]{1,0:T(2,128)S(1)}, /*index=5*/s32[]{:T(128)}) while((s32[]{:T(128)}, f32[81,128,128]{2,1,0:T(8,128)}, s32[2,8]{1,0:T(2,128)S(1)}, bf16[2,256,1024]{2,1,0:T(8,128)(2,1)S(1)}, ...), condition=%wide.region_14.15_spmd, body=%wide.region_12.14_spmd.sunk | while | flops 538706176 | bytes 20976368 | solution.py:136
  118.9 2.8 %fusion.91 = f32[8,128,8,128]{3,1,2,0:T(8,128)} fusion(bf16[8,128,256,1]{2,1,3,0:T(8,128)(2,1)S(1)} %bitcast.168, bf16[8,128,256,1]{2,1,0,3:T(8,128)(2,1)S(1)} %bitcast.169), kind=kOutput, calls=%fused_computation.126.clone.1 | convolution fusion | flops 536870912 | bytes 5242880 | tf_op jit(solution)/shard_map/while/body/eval_jaxpr/dot_general | solution.py:129
  121.8 13.7 %scatter_fusion = f32[81,128,128]{2,1,0:T(8,128)} fusion(f32[81,128,128]{2,1,0:T(8,128)} %get-tuple-element.225, s32[64]{0:T(128)S(1)} %fusion.90, f32[64,128,128]{2,1,0:T(8,128)} %bitcast.166), kind=kCustom, calls=%fused_computation.2.clone.1 | custom fusion | flops 1048576 | bytes 12583168 | tf_op jit(solution)/shard_map/while/body/eval_jaxpr/scatter-add | solution.py:134
  135.9 2.8 %fusion.91 = f32[8,128,8,128]{3,1,2,0:T(8,128)} fusion(bf16[8,128,256,1]{2,1,3,0:T(8,128)(2,1)S(1)} %bitcast.168, bf16[8,128,256,1]{2,1,0,3:T(8,128)(2,1)S(1)} %bitcast.169), kind=kOutput, calls=%fused_computation.126.clone.1 | convolution fusion | flops 536870912 | bytes 5242880 | tf_op jit(solution)/shard_map/while/body/eval_jaxpr/dot_general | solution.py:129
  138.8 13.7 %scatter_fusion = f32[81,128,128]{2,1,0:T(8,128)} fusion(f32[81,128,128]{2,1,0:T(8,128)} %get-tuple-element.225, s32[64]{0:T(128)S(1)} %fusion.90, f32[64,128,128]{2,1,0:T(8,128)} %bitcast.166), kind=kCustom, calls=%fused_computation.2.clone.1 | custom fusion | flops 1048576 | bytes 12583168 | tf_op jit(solution)/shard_map/while/body/eval_jaxpr/scatter-add | solution.py:134
  152.5 3.0 %convert_element_type.34 = bf16[81,128,128]{2,1,0:T(8,128)(2,1)S(1)} convert(f32[81,128,128]{2,1,0:T(8,128)} %get-tuple-element.58) | non-fusion elementwise | flops 1327104 | bytes 7962624 | tf_op jit(solution)/shard_map/convert_element_type | solution.py:144
  155.5 2.9 %broadcast_in_dim.40 = bf16[124,128,128]{2,1,0:T(8,128)(2,1)} broadcast(bf16[]{:T(256)} %constant.117.clone.1), dimensions={} | broadcast | bytes 4063234 | tf_op jit(solution)/shard_map/broadcast_in_dim | solution.py:142
  158.5 12.7 %scatter_fusion.1 = bf16[124,128,128]{2,1,0:T(8,128)(2,1)} fusion(bf16[124,128,128]{2,1,0:T(8,128)(2,1)} %broadcast_in_dim.40, s32[81]{0:T(128)S(1)} %fusion.58, bf16[81,128,128]{2,1,0:T(8,128)(2,1)S(1)} %convert_element_type.34), kind=kCustom, calls=%fused_computation.4 | custom fusion | bytes 7962948 | tf_op jit(solution)/shard_map/scatter | solution.py:144
  171.2 4.8 %all-to-all-start.1 = ((bf16[124,128,128]{2,1,0:T(8,128)(2,1)}), bf16[124,128,128]{2,1,0:T(8,128)(2,1)}, u32[]{:S(2)}, u32[]{:S(2)}) async-start(bf16[124,128,128]{2,1,0:T(8,128)(2,1)} %scatter_fusion.1), calls=%async_computation.1 | async-start | bytes 8126464 | tf_op jit(solution)/shard_map/all_to_all | solution.py:146
  178.4 43.2 %all-to-all-done.1 = bf16[124,128,128]{2,1,0:T(8,128)(2,1)} async-done(((bf16[124,128,128]{2,1,0:T(8,128)(2,1)}), bf16[124,128,128]{2,1,0:T(8,128)(2,1)}, u32[]{:S(2)}, u32[]{:S(2)}) %all-to-all-start.1) | async-done | bytes 4063264 | tf_op jit(solution)/shard_map/all_to_all | solution.py:146
  221.6 6.8 %copy.53 = bf16[124,128,128]{0,2,1:T(8,128)(2,1)} copy(bf16[124,128,128]{2,1,0:T(8,128)(2,1)} %all-to-all-done.1) | data formatting | bytes 8126464 | tf_op jit(solution)/shard_map/reshape | solution.py:152
  228.4 3.7 %fusion.20 = bf16[32,128,128]{2,0,1:T(8,128)(2,1)S(1)} fusion(bf16[124,128,128]{0,2,1:T(8,128)(2,1)} %copy.53, s32[124]{0:T(128)S(1)} %eq.53), kind=kOutput, calls=%fused_computation.36 | convolution fusion | flops 130551680 | bytes 5112304 | tf_op jit(solution)/shard_map/dot_general | solution.py:150
  (89 shorter events, 26.8 us)
Async XLA Ops:
  7.2 58.1 %all-gather.2.cloned.1.call-start = ((), (), s32[]{:S(2)}) async-start(), calls=%async_computation.2 | async-start | bytes 5242880 | tf_op jit(solution)/shard_map/all_gather | solution.py:74
  11.9 159.3 %all-to-all-start = ((s32[4,31,1]{1,2,0:T(1,128)}), s32[4,31,1]{1,2,0:T(1,128)S(1)}, u32[]{:S(2)}, u32[]{:S(2)}) async-start(s32[4,31,1]{1,2,0:T(1,128)} %bitcast.44), calls=%async_computation | async-start | bytes 4096 | tf_op jit(solution)/shard_map/all_to_all | solution.py:72
  68.5 1.8 copy-start.5
  73.2 1.4 copy-start.1
  78.3 1.4 copy-start.1
  80.6 5.9 %copy-start.6 = (s32[2,4]{1,0:T(2,128)S(1)}, s32[2,4]{1,0:T(2,128)}, u32[]{:S(2)}) copy-start(s32[2,4]{1,0:T(2,128)} %param.21) | copy-start | bytes 100
  80.6 30.2 %copy-start = (f32[2,4,256,256]{2,3,1,0:T(8,128)S(1)}, f32[2,4,256,256]{2,3,1,0:T(8,128)}, u32[]{:S(2)}) copy-start(f32[2,4,256,256]{2,3,1,0:T(8,128)} %get-tuple-element.115) | copy-start | bytes 6291460
  86.5 28.4 %copy-start.3 = (f32[2,256,256]{1,2,0:T(8,128)S(1)}, f32[2,256,256]{1,2,0:T(8,128)}, u32[]{:S(2)}) copy-start(f32[2,256,256]{1,2,0:T(8,128)} %get-tuple-element.117) | copy-start | bytes 1572868
  86.5 28.4 %copy-start.4 = (f32[2,256,256]{1,2,0:T(8,128)S(1)}, f32[2,256,256]{1,2,0:T(8,128)}, u32[]{:S(2)}) copy-start(f32[2,256,256]{1,2,0:T(8,128)} %get-tuple-element.118) | copy-start | bytes 1572868
  115.5 3.0 %copy-start.2 = (bf16[2,256,1024]{2,1,0:T(8,128)(2,1)S(1)}, bf16[2,256,1024]{2,1,0:T(8,128)(2,1)}, u32[]{:S(2)}) copy-start(bf16[2,256,1024]{2,1,0:T(8,128)(2,1)} %get-tuple-element.239) | copy-start | bytes 3145732
  171.2 50.4 %all-to-all-start.1 = ((bf16[124,128,128]{2,1,0:T(8,128)(2,1)}), bf16[124,128,128]{2,1,0:T(8,128)(2,1)}, u32[]{:S(2)}, u32[]{:S(2)}) async-start(bf16[124,128,128]{2,1,0:T(8,128)(2,1)} %scatter_fusion.1), calls=%async_computation.1 | async-start | bytes 8126464 | tf_op jit(solution)/shard_map/all_to_all | solution.py:146
Sparse Core Ops, SparseCore 0:
  9.8 55.4 all-gather.1
where the time goes:
time: 242 us; the launch traced here: 240 us
  waiting for transfers between devices  69.1 us (29%)
  local copies, waits for them, and re-layouts  43.4 us (18%)
  matrix products  40.2 us (17%)
  other arithmetic  39.7 us (16%)
  blocking collectives  23.5 us (10%)
  between operations  14.2 us (6%)
  starting transfers between devices  10 us (4%)
    all_to_all x1, waiting for transfers between devices, on_device(): lax.all_to_all(ham_out, 'dev', split_axis=0, concat_axis=0, tiled=True)  43.2 us
    scatter-add x2, other arithmetic, hamilton_step(): return (ham_local.at[block_index].add(pieces), None)  27.4 us
    all_gather x1, waiting for transfers between devices, on_device(): portion = lax.all_gather(dens_tiles, 'dev', axis=0, tiled=True)  25.2 us
    psum x1, blocking collectives, on_device(): lax.psum(jnp.dot(moments_grp[:, 0], atom_trig, precision=TOP_PRECISION),...  14.3 us
    scatter x1, local copies, waits for them, and re-layouts, on_device(): ham_out = jnp.zeros((owner_count * capacity, TB, TB), jnp.bfloat16).at[se...  12.7 us
    dot_general x1, matrix products, local_basis(): jnp.einsum('cbnp,cm->bnpm', displace, wave_vecs, precision=TOP_PRECISION)  12.3 us
    psum x1, blocking collectives, on_device(): moments_grp = lax.psum(moments_dev, 'dev')  9.19 us
    gather x4, local copies, waits for them, and re-layouts, density_step(): local_tiles[block_index].transpose(0, 2, 1, 3).reshape(BB * TB, BB * TB)  8.14 us
  transfers between devices with their start and end apart: 3, of which 2 were waited for; matrix products, arithmetic and copies ran while one was open for 46% of the time, Pallas kernels for 0%

commit v1 on v0

v1 whole, which is shorter than its diff:
```python
import functools
import math

import jax
import jax.numpy as jnp
from jax import lax
from jax.experimental import pallas as pl
from jax.experimental.pallas import tpu as pltpu
from jax.sharding import PartitionSpec as P

TB = 128
KM = 512
GRIDN = 64
HALF = KM // 2
MESH = pl.DeviceIdType.MESH
TOP = lax.Precision.HIGHEST
VM = pl.BlockSpec(memory_space=pltpu.VMEM)
SM = pl.BlockSpec(memory_space=pltpu.SMEM)
ANY = pl.BlockSpec(memory_space=pl.ANY)


def modes(shape, axis):
    k = lax.broadcasted_iota(jnp.int32, shape, axis)
    return tuple(v.astype(jnp.float32) for v in (k & 7, (k >> 3) & 7, k >> 6))


def turn_trig(turns):
    angle = (turns - jnp.round(turns)) * (2.0 * math.pi)
    return jnp.cos(angle), jnp.sin(angle)


def gather_kernel(
    n, orb, meta, coords, atoms_s, weights_s, grid_s,
    orb_all, meta_all, table, phase, spread,
    turns, own_sem, send, recv, msend, mrecv,
):
    me = lax.axis_index("dev")
    bits = n.bit_length() - 1
    batches, points = orb.shape[0], orb.shape[1]
    barrier = pltpu.get_barrier_semaphore()
    for step in range(1, n):
        pl.semaphore_signal(
            barrier, inc=1, device_id={"dev": lax.rem(me + step, n)}, device_id_type=MESH
        )
    pl.semaphore_wait(barrier, n - 1)

    def order_of(b):
        return list(range(bits)) if b % 2 == 0 else list(range(bits))[::-1]

    def block_copy(b, stage, mask):
        source = me ^ mask
        bit = 1 << order_of(b)[stage]
        got = mask ^ bit
        return pltpu.make_async_remote_copy(
            src_ref=orb.at[b] if mask == 0 else orb_all.at[source, b],
            dst_ref=orb_all.at[source, b],
            send_sem=send.at[b, got],
            recv_sem=recv.at[b, got],
            device_id={"dev": me ^ bit},
            device_id_type=MESH,
        )

    started = []
    metas = []
    for step in range(1, n):
        metas.append(
            pltpu.make_async_remote_copy(
                src_ref=meta,
                dst_ref=meta_all.at[me],
                send_sem=msend.at[step - 1],
                recv_sem=mrecv.at[step - 1],
                device_id={"dev": lax.rem(me + step, n)},
                device_id_type=MESH,
            )
        )
        metas[-1].start()
    for stage in range(bits):
        for b in range(batches):
            copy = block_copy(b, stage, 0)
            copy.start()
            started.append(copy)
    own = [
        pltpu.make_async_copy(orb, orb_all.at[me], own_sem.at[0]),
        pltpu.make_async_copy(meta, meta_all.at[me], own_sem.at[1]),
    ]
    for copy in own:
        copy.start()

    rows = 32

    def table_rows(c, carry):
        shape = (rows, batches * points)
        k = lax.broadcasted_iota(jnp.int32, shape, 0) + c * rows
        fx, fy, fz = (v.astype(jnp.float32) for v in (k & 7, (k >> 3) & 7, k >> 6))
        at = fx * coords[0:1, :] + fy * coords[1:2, :] + fz * coords[2:3, :]
        cos, sin = turn_trig(at * (1.0 / GRIDN))
        table[pl.ds(pl.multiple_of(c * rows, rows), rows), :] = cos
        table[pl.ds(pl.multiple_of(HALF + c * rows, rows), rows), :] = sin
        return carry

    def small_tables():
        atoms = grid_s.shape[1]
        turns[...] = jnp.zeros_like(turns)
        spread[...] = jnp.zeros_like(spread)
        fx, fy, fz = modes((1, HALF), 1)
        for a in range(atoms):
            place = [grid_s[c, a].astype(jnp.float32) for c in range(3)]
            turns[a : a + 1, :] = (fx * place[0] + fy * place[1] + fz * place[2]) * (1.0 / GRIDN)
            for b in range(batches):
                cols = slice(b * points, (b + 1) * points)
                share, total = jnp.int32(0), jnp.int32(0)
                for near in range(atoms_s.shape[1]):
                    weight = weights_s[b, near]
                    share = share + jnp.where(atoms_s[b, near] == a, weight, 0)
                    total = total + weight
                gone = [coords[c : c + 1, cols] - place[c] for c in range(3)]
                squared = gone[0] * gone[0] + gone[1] * gone[1] + gone[2] * gone[2]
                part = jnp.full((1, points), share.astype(jnp.float32)) / jnp.full(
                    (1, points), total.astype(jnp.float32)
                )
                spread[a : a + 1, cols] = part * jnp.exp(squared * (-2.0 / (GRIDN * GRIDN)))
        cos, sin = turn_trig(turns[...])
        phase[0] = cos
        phase[1] = sin

    small_tables()
    half_chunks = HALF // rows // 2
    lax.fori_loop(0, half_chunks, table_rows, 0)
    for stage in range(bits):
        for b in range(batches):
            for low in range(1 << stage):
                got = 1 << order_of(b)[stage]
                for t in range(stage):
                    if low >> t & 1:
                        got ^= 1 << order_of(b)[t]
                arrival = orb_all.at[me ^ got, b]
                pltpu.make_async_remote_copy(
                    src_ref=arrival,
                    dst_ref=arrival,
                    send_sem=send.at[b, got],
                    recv_sem=recv.at[b, got],
                    device_id={"dev": me ^ (1 << order_of(b)[stage])},
                    device_id_type=MESH,
                ).wait_recv()
                for later in range(stage + 1, bits):
                    copy = block_copy(b, later, got)
                    copy.start()
                    started.append(copy)
        if stage == 0:
            lax.fori_loop(half_chunks, HALF // rows, table_rows, 0)
    for copy in started:
        copy.wait_send()
    for copy in metas:
        copy.wait()
    for copy in own:
        copy.wait()


def density_kernel(meta, orb, dens, out, tiles, block, sem):
    e = pl.program_id(0)
    me = lax.axis_index("dev")
    stored = dens.shape[0]
    batches, points, width = orb.shape[1:]
    blocks = width // TB

    @pl.when(e == 0)
    def _():
        tiles[stored] = jnp.zeros((TB, TB), jnp.bfloat16)
        copy = pltpu.make_async_copy(dens, tiles.at[pl.ds(0, stored)], sem)
        copy.start()
        copy.wait()

    union = meta[0, 2, 0]
    for b in range(batches):

        def row(i, carry):
            ci = meta[e, 1, b * blocks + i]
            for j in range(blocks):
                code = meta[e, 0, ci * union + meta[e, 1, b * blocks + j]] - me * stored
                index = jnp.where((code >= 0) & (code < stored), code, stored)
                block[pl.ds(pl.multiple_of(i * TB, TB), TB), j * TB : (j + 1) * TB] = tiles[index]
            return carry

        lax.fori_loop(0, blocks, row, 0)
        total = jnp.zeros((points, TB), jnp.float32)
        for c in range(width // (2 * TB)):
            cols = slice(2 * c * TB, 2 * (c + 1) * TB)
            product = jnp.dot(orb[0, b], block[:, cols], preferred_element_type=jnp.float32)
            product = product * orb[0, b, :, cols].astype(jnp.float32)
            total = total + product[:, :TB] + product[:, TB:]
        line = jnp.sum(total.T, axis=0, keepdims=True)
        out[0, :, b * points : (b + 1) * points] = jnp.broadcast_to(line, (8, points))


def field_kernel(
    n, regions, dens, weights, table, phase, spread,
    density, potential, scaled_all,
    dens_in, terms, terms_in, struct, struct_in, scaled,
    dsend, drecv, tsend, trecv, ssend, srecv, psend, precv, own_sem,
):
    me = lax.axis_index("dev")
    grp = lax.axis_index("grp")
    barrier = pltpu.get_barrier_semaphore()
    for step in range(1, n):
        pl.semaphore_signal(
            barrier, inc=1, device_id={"dev": lax.rem(me + step, n)}, device_id_type=MESH
        )
    for step in range(1, regions):
        pl.semaphore_signal(
            barrier, inc=1, device_id={"grp": lax.rem(grp + step, regions)}, device_id_type=MESH
        )
    pl.semaphore_wait(barrier, n + regions - 2)

    def send_all(axis, count, src_of, dst_of, ssem, rsem):
        here = me if axis == "dev" else grp
        copies = []
        for step in range(1, count):
            peer = lax.rem(here + step, count)
            copies.append(
                pltpu.make_async_remote_copy(
                    src_ref=src_of(peer),
                    dst_ref=dst_of(step - 1),
                    send_sem=ssem.at[step - 1],
                    recv_sem=rsem.at[step - 1],
                    device_id={axis: peer},
                    device_id_type=MESH,
                )
            )
            copies[-1].start()
        return copies

    copies = send_all("dev", n, lambda peer: dens.at[peer], lambda s: dens_in.at[s], dsend, drecv)
    cos, sin = phase[0], phase[1]
    fx, fy, fz = modes((1, HALF), 1)
    squared = fx * fx + fy * fy + fz * fz
    near_gain = 0.1 / (1.0 + 0.1 * squared)
    far_gain = 0.03 / (1.0 + 0.1 * squared)
    rho = dens[me]
    for s, copy in enumerate(copies):
        copy.wait()
        rho = rho + dens_in[s]
    density[...] = rho
    source = spread[...] * (weights[...] * rho[0:1, :])
    mine = lax.dot_general(
        source, table[...], (((1,), (1,)), ((), ())), precision=TOP,
        preferred_element_type=jnp.float32,
    )
    terms[...] = mine
    copies = send_all("dev", n, lambda peer: terms, lambda s: terms_in.at[s], tsend, trecv)
    for s, copy in enumerate(copies):
        copy.wait()
        mine = mine + terms_in[s]
    even, odd = mine[:, :HALF], mine[:, HALF:]
    even, odd = even * cos + odd * sin, odd * cos - even * sin
    charge = even[:, 0:1]
    mine_struct = jnp.concatenate(
        [
            jnp.sum(charge * cos, axis=0, keepdims=True),
            jnp.sum(charge * sin, axis=0, keepdims=True),
        ],
        axis=1,
    )
    total = jnp.broadcast_to(mine_struct, (8, KM))
    struct[...] = total
    copies = send_all("grp", regions, lambda peer: struct, lambda s: struct_in.at[s], ssend, srecv)
    even, odd = even * near_gain, odd * near_gain
    coef = jnp.concatenate([even * cos - odd * sin, even * sin + odd * cos], axis=1)
    value = jnp.dot(coef, table[...], precision=TOP, preferred_element_type=jnp.float32)
    near = jnp.sum(value * spread[...], axis=0, keepdims=True)
    for s, copy in enumerate(copies):
        copy.wait()
        total = total + struct_in[s]
    far_coef = total * jnp.concatenate([far_gain, far_gain], axis=1)
    far = jnp.dot(far_coef, table[...], precision=TOP, preferred_element_type=jnp.float32)
    field = near + far
    potential[...] = field
    scaled[...] = weights[...] * field
    own = pltpu.make_async_copy(scaled, scaled_all.at[me], own_sem)
    own.start()
    copies = []
    for step in range(1, n):
        copies.append(
            pltpu.make_async_remote_copy(
                src_ref=scaled,
                dst_ref=scaled_all.at[me],
                send_sem=psend.at[step - 1],
                recv_sem=precv.at[step - 1],
                device_id={"dev": lax.rem(me + step, n)},
                device_id_type=MESH,
            )
        )
        copies[-1].start()
    for copy in copies:
        copy.wait()
    own.wait()


def hamilton_kernel(meta, orb, scaled, out, total, scaled_orb, block):
    e = pl.program_id(0)
    me = lax.axis_index("dev")
    stored = out.shape[0]
    batches, points, width = orb.shape[1:]
    blocks = width // TB

    @pl.when(e == 0)
    def _():
        total[...] = jnp.zeros_like(total)

    union = meta[0, 2, 0]
    for b in range(batches):
        line = scaled[0, 0:1, b * points : (b + 1) * points]
        column = jnp.broadcast_to(line, (TB, points)).T
        for j in range(blocks):
            cols = slice(j * TB, (j + 1) * TB)
            scaled_orb[:, cols] = (column * orb[0, b, :, cols].astype(jnp.float32)).astype(
                jnp.bfloat16
            )
        for c in range(width // (2 * TB)):
            cols = slice(2 * c * TB, 2 * (c + 1) * TB)
            block[:, cols] = lax.dot_general(
                orb[0, b], scaled_orb[:, cols], (((0,), (0,)), ((), ())),
                preferred_element_type=jnp.float32,
            )

        def row(i, carry):
            ci = meta[e, 1, b * blocks + i]
            for j in range(blocks):
                code = meta[e, 0, ci * union + meta[e, 1, b * blocks + j]] - me * stored

                @pl.when((code >= 0) & (code < stored))
                def _():
                    piece = block[pl.ds(pl.multiple_of(i * TB, TB), TB), j * TB : (j + 1) * TB]
                    total[code] = total[code] + piece

            return carry

        lax.fori_loop(0, blocks, row, 0)

    @pl.when(e == pl.num_programs(0) - 1)
    def _():
        out[...] = total[...].astype(jnp.bfloat16)


def on_device(
    n, regions, orbitals, dens_tiles, point_coords, point_weights, batch_blocks,
    tile_owner, tile_slot, batch_atoms, batch_weights, atom_grid_index,
):
    stored = dens_tiles.shape[0]
    listed = tile_slot.shape[0]
    batches, points, width = orbitals.shape
    here = batches * points
    rows = -(-atom_grid_index.shape[1] // 8) * 8
    code = tile_owner[:, 0] * stored + tile_slot
    meta = jnp.concatenate(
        [
            jnp.pad(code, (0, TB - listed))[None],
            jnp.pad(batch_blocks.reshape(-1), (0, TB - batch_blocks.size))[None],
            jnp.full((6, TB), math.isqrt(listed), jnp.int32),
        ]
    )
    f32, i32, bf16 = jnp.float32, jnp.int32, jnp.bfloat16
    S = jax.ShapeDtypeStruct
    dma = pltpu.SemaphoreType.DMA
    orb_all, meta_all, table, phase, spread = pl.pallas_call(
        functools.partial(gather_kernel, n),
        out_shape=(
            S((n, batches, points, width), bf16),
            S((n, 8, TB), i32),
            S((KM, here), f32),
            S((2, rows, HALF), f32),
            S((rows, here), f32),
        ),
        in_specs=[VM, VM, VM, SM, SM, SM],
        out_specs=(ANY, ANY, VM, VM, VM),
        scratch_shapes=[
            pltpu.VMEM((rows, HALF), f32),
            dma((2,)),
            dma((batches, n)),
            dma((batches, n)),
            dma((n,)),
            dma((n,)),
        ],
        compiler_params=pltpu.CompilerParams(collective_id=0, has_side_effects=True),
        name="gather",
    )(orbitals, meta, point_coords, batch_atoms, batch_weights, atom_grid_index)
    orb_spec = pl.BlockSpec((1, batches, points, width), lambda e: (e, 0, 0, 0))
    row_spec = pl.BlockSpec((1, 8, here), lambda e: (e, 0, 0))
    dens_part = pl.pallas_call(
        density_kernel,
        grid=(n,),
        out_shape=S((n, 8, here), f32),
        in_specs=[SM, orb_spec, ANY],
        out_specs=row_spec,
        scratch_shapes=[
            pltpu.VMEM((stored + 1, TB, TB), bf16),
            pltpu.VMEM((width, width), bf16),
            dma,
        ],
        name="density",
    )(meta_all, orb_all, dens_tiles)
    density, potential, scaled_all = pl.pallas_call(
        functools.partial(field_kernel, n, regions),
        out_shape=(S((8, here), f32), S((8, here), f32), S((n, 8, here), f32)),
        in_specs=[VM] * 5,
        out_specs=(VM, VM, VM),
        scratch_shapes=[
            pltpu.VMEM((n, 8, here), f32),
            pltpu.VMEM((rows, KM), f32),
            pltpu.VMEM((n, rows, KM), f32),
            pltpu.VMEM((8, KM), f32),
            pltpu.VMEM((regions, 8, KM), f32),
            pltpu.VMEM((8, here), f32),
            dma((n,)), dma((n,)), dma((n,)), dma((n,)),
            dma((regions,)), dma((regions,)), dma((n,)), dma((n,)), dma,
        ],
        compiler_params=pltpu.CompilerParams(collective_id=1, has_side_effects=True),
        name="field",
    )(dens_part, point_weights.reshape(1, here), table, phase, spread)
    ham_tiles = pl.pallas_call(
        hamilton_kernel,
        grid=(n,),
        out_shape=S((stored, TB, TB), bf16),
        in_specs=[SM, orb_spec, row_spec],
        out_specs=VM,
        scratch_shapes=[
            pltpu.VMEM((stored, TB, TB), f32),
            pltpu.VMEM((points, width), bf16),
            pltpu.VMEM((width, width), f32),
        ],
        name="hamilton",
    )(meta_all, orb_all, scaled_all)
    return density[0], potential[0], ham_tiles


def solution(mesh):
    body = functools.partial(on_device, mesh.shape["dev"], mesh.shape["grp"])
    in_specs = (
        P(("grp", "dev"), None, None),
        P(("grp", "dev"), None, None),
        P(None, ("grp", "dev")),
        P(("grp", "dev")),
        P(("grp", "dev"), None),
        P(("grp", "dev"), None),
        P(("grp", "dev")),
        P(("grp", "dev"), None),
        P(("grp", "dev"), None),
        P(None, "grp"),
    )
    out_specs = (P(("grp", "dev")), P(("grp", "dev")), P(("grp", "dev"), None, None))
    return jax.shard_map(body, mesh=mesh, in_specs=in_specs, out_specs=out_specs, check_vma=False)
```

time: 242 us -> 102 us (0.42)
  Pallas kernels: 0 us -> 96.6 us
  waiting for transfers between devices: 69.1 us -> 0 us
  matrix products: 40.2 us -> 0 us
  local copies, waits for them, and re-layouts: 43.4 us -> 3.43 us
  other arithmetic: 39.7 us -> 1.34 us
  blocking collectives: 23.5 us -> 0 us
  between operations: 14.2 us -> 0.66 us
  starting transfers between devices: 10 us -> 0 us
    pallas_call x0 -> x4, Pallas kernels: none -> 96.6 us  [the longest x1 41.4 us: on_device(): pl.pallas_call(functools.partial(gather_kernel, n), out_shape=(S((n, batc...]
    all_to_all x2 -> x0, waiting for transfers between devices: 43.2 us -> none  [the longest x1 43.2 us: on_device(): lax.all_to_all(ham_out, 'dev', split_axis=0, concat_axis=0, tiled=True)]
    dot_general x15 -> x0, matrix products: 40.2 us -> none  [the longest x1 12.3 us: local_basis(): jnp.einsum('cbnp,cm->bnpm', displace, wave_vecs, precision=TOP_PRECISION)]
    scatter-add x2 -> x0, other arithmetic: 27.4 us -> none  [hamilton_step(): return (ham_local.at[block_index].add(pieces), None)]
    all_gather x1 -> x0, waiting for transfers between devices: 25.2 us -> none  [on_device(): portion = lax.all_gather(dens_tiles, 'dev', axis=0, tiled=True)]
    psum x2 -> x0, blocking collectives: 23.5 us -> none  [the longest x1 14.3 us: on_device(): lax.psum(jnp.dot(moments_grp[:, 0], atom_trig, precision=TOP_PRECISION),...]
    scatter x2 -> x0, local copies, waits for them, and re-layouts: 13.7 us -> none  [the longest x1 12.7 us: on_device(): ham_out = jnp.zeros((owner_count * capacity, TB, TB), jnp.bfloat16).at[se...]
    gather x5 -> x0, local copies, waits for them, and re-layouts: 11.4 us -> none  [the longest x4 8.14 us: density_step(): local_tiles[block_index].transpose(0, 2, 1, 3).reshape(BB * TB, BB * TB)]
  transfers between devices with their start and end apart: 3 -> 0, of which waited for: 2 -> 0; matrix products, arithmetic and copies ran while one was open for 46% -> 0% of each run, Pallas kernels for 0% -> 0%
where the time goes in v1:
time: 102 us
  Pallas kernels  96.6 us (95%)
  local copies, waits for them, and re-layouts  3.43 us (3%)
  other arithmetic  1.34 us (1%)
    pallas_call x1, Pallas kernels, on_device(): pl.pallas_call(functools.partial(gather_kernel, n), out_shape=(S((n, batc...  41.4 us
    pallas_call x1, Pallas kernels, on_device(): pl.pallas_call(functools.partial(field_kernel, n, regions), out_shape=(S(...  20.7 us
    pallas_call x1, Pallas kernels, on_device(): pl.pallas_call(hamilton_kernel, grid=(n,), out_shape=S((stored, TB, TB),...  19.5 us
    pallas_call x1, Pallas kernels, on_device(): pl.pallas_call(density_kernel, grid=(n,), out_shape=S((n, 8, here), f32),...  15 us
    slice x2, local copies, waits for them, and re-layouts, on_device(): return (density[0], potential[0], ham_tiles)  2.59 us

profile of v1, /device:TPU:0, one launch (start us, length us, event | category | flops | bytes accessed | tf_op | source)
XLA Modules:
  0.0 102.0 jit_solution(3265149518809280017)
XLA Ops:
  0.6 0.8 reshape.14
  1.4 0.7 bitcast_add_fusion
  2.1 0.1 pad.12.clone
  2.1 0.7 add_add_fusion.meta
  2.8 41.4 %gather.1 = (bf16[4,2,256,1024]{3,2,1,0:T(8,128)(2,1)}, s32[4,8,128]{2,1,0:T(8,128)}, f32[512,512]{1,0:T(8,128)}, f32[2,8,256]{2,1,0:T(8,128)}, f32[8,512]{1,0:T(8,128)}) custom-call(bf16[2,256,1024]{2,1,0:T(8,128)(2,1)} %orb.1, s32[8,128]{1,0:T(8,128)} %add_add_fusion.meta, f32[3,512]{1,0:T(4,128)} %coords.1, s32[2,4]{1,0:T(2,128)} %atoms_s.1, ...), custom_call_target="tpu_custom_call" | custom-call | tf_op jit(solution)/shard_map/gather/pallas_call | solution.py:364
  44.2 15.0 %density.1.dens = f32[4,8,512]{2,1,0:T(8,128)} custom-call(s32[4,8,128]{2,1,0:T(8,128)} %get-tuple-element.11.meta, bf16[4,2,256,1024]{3,2,1,0:T(8,128)(2,1)} %get-tuple-element.12.orb, bf16[32,128,128]{2,1,0:T(8,128)(2,1)} %dens.1), custom_call_target="tpu_custom_call" | custom-call | tf_op jit(solution)/shard_map/density/pallas_call | solution.py:388
  59.2 20.7 %field.1 = (f32[8,512]{1,0:T(8,128)}, f32[8,512]{1,0:T(8,128)}, f32[4,8,512]{2,1,0:T(8,128)}) custom-call(f32[4,8,512]{2,1,0:T(8,128)} %density.1.dens, f32[1,512]{1,0:T(1,128)} %bitcast.9, f32[512,512]{1,0:T(8,128)} %get-tuple-element.13.table, f32[2,8,256]{2,1,0:T(8,128)} %get-tuple-element.14.phase, f32[8,512]{1,0:T(8,128)} %get-tuple-element.15.spread), custom_call_target="tpu_custom_call" | custom-call | tf_op jit(solution)/shard_map/field/pallas_call | solution.py:401
  79.9 19.5 %hamilton.1 = bf16[32,128,128]{2,1,0:T(8,128)(2,1)} custom-call(s32[4,8,128]{2,1,0:T(8,128)} %get-tuple-element.11.meta, bf16[4,2,256,1024]{3,2,1,0:T(8,128)(2,1)} %get-tuple-element.12.orb, f32[4,8,512]{2,1,0:T(8,128)} %get-tuple-element.18.scaled), custom_call_target="tpu_custom_call" | custom-call | tf_op jit(solution)/shard_map/hamilton/pallas_call | solution.py:419
  99.4 1.3 %slice.6 = f32[1,512]{1,0:T(1,128)} slice(f32[8,512]{1,0:T(8,128)} %get-tuple-element.16), slice={[0:1], [0:512]} | slice | bytes 4096 | tf_op jit(solution)/shard_map/slice | solution.py:432
  100.7 1.3 %slice.7 = f32[1,512]{1,0:T(1,128)} slice(f32[8,512]{1,0:T(8,128)} %get-tuple-element.17), slice={[0:1], [0:512]} | slice | bytes 4096 | tf_op jit(solution)/shard_map/slice | solution.py:432
  (2 shorter events, 0.0 us)

commit v2 on v1

v2 whole, which is shorter than its diff:
```python
import functools
import math

import jax
import jax.numpy as jnp
from jax import lax
from jax.experimental import pallas as pl
from jax.experimental.pallas import tpu as pltpu
from jax.sharding import PartitionSpec as P

TB = 128
KM = 512
GRIDN = 64
HALF = KM // 2
MESH = pl.DeviceIdType.MESH
TOP = lax.Precision.HIGHEST
VM = pl.BlockSpec(memory_space=pltpu.VMEM)
SM = pl.BlockSpec(memory_space=pltpu.SMEM)
ANY = pl.BlockSpec(memory_space=pl.ANY)


def modes(shape, axis):
    k = lax.broadcasted_iota(jnp.int32, shape, axis)
    return tuple(v.astype(jnp.float32) for v in (k & 7, (k >> 3) & 7, k >> 6))


def turn_trig(turns):
    angle = (turns - jnp.round(turns)) * (2.0 * math.pi)
    return jnp.cos(angle), jnp.sin(angle)


def region_kernel(
    n, regions, orb, meta, coords, weights, dens, atoms_s, weights_s, grid_s,
    density, potential, scaled_all, meta_all, union_all, flip_all,
    table, phase, spread, turns, tiles, block, union, flip, part, part_in,
    terms, terms_in, struct, struct_in, scaled, meta_s,
    pack_sem, local_sem, send, recv, msend, mrecv, dsend, drecv, tsend, trecv, ssend, srecv, psend, precv,
    usem, fsem, *land,
):
    me = lax.axis_index("dev")
    grp = lax.axis_index("grp")
    bits = n.bit_length() - 1
    batches, points, width = orb.shape
    stored = dens.shape[0]
    blocks = union.shape[2] // TB
    held = width // TB
    packs = []
    for b in range(batches):
        for u in range(held):
            copy = pltpu.make_async_copy(
                orb.at[b, :, pl.ds(u * TB, TB)], land[0].at[b, u], pack_sem.at[b, u]
            )
            copy.start()
            packs.append(copy)
    for ref in land:
        for b in range(batches):
            ref[b, held] = jnp.zeros((points, TB), jnp.bfloat16)

    def clear(t, carry):
        tiles[t] = jnp.zeros((TB, TB), jnp.bfloat16)
        return carry

    lax.fori_loop(0, n * stored, clear, 0)
    for copy in packs:
        copy.wait()
    barrier = pltpu.get_barrier_semaphore()
    for mask in range(1, n):
        pl.semaphore_signal(barrier, inc=1, device_id={"dev": me ^ mask}, device_id_type=MESH)
    for step in range(1, regions):
        pl.semaphore_signal(
            barrier, inc=1, device_id={"grp": lax.rem(grp + step, regions)}, device_id_type=MESH
        )
    pl.semaphore_wait(barrier, n + regions - 2)

    def remote(src, dst, ssem, rsem, **where):
        return pltpu.make_async_remote_copy(
            src_ref=src, dst_ref=dst, send_sem=ssem, recv_sem=rsem,
            device_id=where, device_id_type=MESH,
        )

    def to_peers(src_of, dst_of, ssem, rsem):
        copies = []
        for mask in range(1, n):
            copy = remote(src_of(mask), dst_of(mask), ssem.at[mask], rsem.at[mask], dev=me ^ mask)
            copy.start()
            copies.append(copy)
        return copies

    def order_of(b):
        return list(range(bits)) if b % 2 == 0 else list(range(bits))[::-1]

    def landing(mask, b):
        return land[mask].at[b, pl.ds(0, held)]

    def block_copy(b, stage, mask):
        bit = 1 << order_of(b)[stage]
        got = mask ^ bit
        return remote(landing(mask, b), landing(got, b), send.at[b, got], recv.at[b, got], dev=me ^ bit)

    started = []
    metas = to_peers(lambda mask: meta, lambda mask: meta_all.at[me], msend, mrecv)
    for stage in range(bits):
        for b in range(batches):
            copy = block_copy(b, stage, 0)
            copy.start()
            started.append(copy)
    own = [
        pltpu.make_async_copy(meta, meta_all.at[me], local_sem.at[0]),
        pltpu.make_async_copy(dens, tiles.at[pl.ds(me * stored, stored)], local_sem.at[1]),
    ]
    for copy in own:
        copy.start()

    rows = 32

    def table_rows(c, carry):
        shape = (rows, batches * points)
        k = lax.broadcasted_iota(jnp.int32, shape, 0) + c * rows
        fx, fy, fz = (v.astype(jnp.float32) for v in (k & 7, (k >> 3) & 7, k >> 6))
        at = fx * coords[0:1, :] + fy * coords[1:2, :] + fz * coords[2:3, :]
        cos, sin = turn_trig(at * (1.0 / GRIDN))
        table[pl.ds(pl.multiple_of(c * rows, rows), rows), :] = cos
        table[pl.ds(pl.multiple_of(HALF + c * rows, rows), rows), :] = sin
        return carry

    def small_tables():
        atoms = grid_s.shape[1]
        turns[...] = jnp.zeros_like(turns)
        spread[...] = jnp.zeros_like(spread)
        fx, fy, fz = modes((1, HALF), 1)
        for a in range(atoms):
            place = [grid_s[c, a].astype(jnp.float32) for c in range(3)]
            turns[a : a + 1, :] = (fx * place[0] + fy * place[1] + fz * place[2]) * (1.0 / GRIDN)
            for b in range(batches):
                cols = slice(b * points, (b + 1) * points)
                share, total = jnp.int32(0), jnp.int32(0)
                for near in range(atoms_s.shape[1]):
                    weight = weights_s[b, near]
                    share = share + jnp.where(atoms_s[b, near] == a, weight, 0)
                    total = total + weight
                gone = [coords[c : c + 1, cols] - place[c] for c in range(3)]
                squared = gone[0] * gone[0] + gone[1] * gone[1] + gone[2] * gone[2]
                fraction = jnp.full((1, points), share.astype(jnp.float32)) / jnp.full(
                    (1, points), total.astype(jnp.float32)
                )
                spread[a : a + 1, cols] = fraction * jnp.exp(squared * (-2.0 / (GRIDN * GRIDN)))
        cos, sin = turn_trig(turns[...])
        phase[0] = cos
        phase[1] = sin

    results = {}
    density_sends = []

    def process(mask):
        e = me ^ mask
        slot = len(results) % 2
        if len(results) >= 2:
            for copy in list(results.values())[-2]:
                copy.wait()
        for b in range(batches):
            at = slice(b * points, (b + 1) * points)
            for u in range(blocks):
                index = meta_s[e, 1, b * blocks + u]
                union[slot, at, u * TB : (u + 1) * TB] = land[mask][b, index]

        def flip_block(u, carry):
            first = pl.multiple_of(u * TB, TB)
            flip[slot, pl.ds(first, TB), :] = union[slot, :, pl.ds(first, TB)].T
            return carry

        lax.fori_loop(0, blocks, flip_block, 0)
        outs = [
            pltpu.make_async_copy(union.at[slot], union_all.at[e], usem.at[mask]),
            pltpu.make_async_copy(flip.at[slot], flip_all.at[e], fsem.at[mask]),
        ]
        for copy in outs:
            copy.start()
        results[mask] = outs

        def row(i, carry):
            for j in range(blocks):
                index = meta_s[e, 0, i * blocks + j]
                block[pl.ds(pl.multiple_of(i * TB, TB), TB), j * TB : (j + 1) * TB] = tiles[index]
            return carry

        lax.fori_loop(0, blocks, row, 0)
        total = jnp.zeros((batches * points, TB), jnp.float32)
        for c in range(0, blocks, 2):
            some = min(2, blocks - c)
            cols = slice(c * TB, (c + some) * TB)
            orbital = union[slot, :, cols]
            product = jnp.dot(union[slot], block[:, cols], preferred_element_type=jnp.float32)
            product = product * orbital.astype(jnp.float32)
            for t in range(some):
                total = total + product[:, t * TB : (t + 1) * TB]
        line = jnp.sum(total.T, axis=0, keepdims=True)
        part[mask] = jnp.broadcast_to(line, (8, batches * points))
        if mask:
            copy = remote(
                part.at[mask], part_in.at[mask], dsend.at[mask], drecv.at[mask], dev=me ^ mask
            )
            copy.start()
            density_sends.append(copy)

    small_tables()
    chunks = HALF // rows
    lax.fori_loop(0, chunks // 2, table_rows, 0)
    for copy in metas + own:
        copy.wait()
    to_smem = pltpu.make_async_copy(meta_all, meta_s, local_sem.at[0])
    to_smem.start()
    to_smem.wait()
    process(0)
    arrived = {}
    for stage in range(bits):
        for low in range(1 << stage):
            for b in range(batches):
                bit = 1 << order_of(b)[stage]
                got = bit
                for t in range(stage):
                    if low >> t & 1:
                        got ^= 1 << order_of(b)[t]
                there = landing(got, b)
                remote(there, there, send.at[b, got], recv.at[b, got], dev=me ^ bit).wait_recv()
                for later in range(stage + 1, bits):
                    copy = block_copy(b, later, got)
                    copy.start()
                    started.append(copy)
                arrived[got] = arrived.get(got, 0) + 1
                if arrived[got] == batches:
                    process(got)
        if stage == 0:
            lax.fori_loop(chunks // 2, chunks, table_rows, 0)

    cos, sin = phase[0], phase[1]
    fx, fy, fz = modes((1, HALF), 1)
    squared = fx * fx + fy * fy + fz * fz
    near_gain = 0.1 / (1.0 + 0.1 * squared)
    far_gain = 0.03 / (1.0 + 0.1 * squared)
    rho = part[0]
    for copy in density_sends:
        copy.wait()
    for mask in range(1, n):
        rho = rho + part_in[mask]
    density[...] = rho
    source = spread[...] * (weights[...] * rho[0:1, :])
    mine = lax.dot_general(
        source, table[...], (((1,), (1,)), ((), ())), precision=TOP,
        preferred_element_type=jnp.float32,
    )
    terms[...] = mine
    copies = to_peers(lambda mask: terms, lambda mask: terms_in.at[mask], tsend, trecv)
    for mask, copy in enumerate(copies, 1):
        copy.wait()
        mine = mine + terms_in[mask]
    even, odd = mine[:, :HALF], mine[:, HALF:]
    even, odd = even * cos + odd * sin, odd * cos - even * sin
    charge = even[:, 0:1]
    total = jnp.concatenate(
        [
            jnp.sum(charge * cos, axis=0, keepdims=True),
            jnp.sum(charge * sin, axis=0, keepdims=True),
        ],
        axis=1,
    )
    total = jnp.broadcast_to(total, (8, KM))
    struct[...] = total
    copies = []
    for step in range(1, regions):
        copies.append(
            remote(
                struct, struct_in.at[step], ssend.at[step], srecv.at[step],
                grp=lax.rem(grp + step, regions),
            )
        )
        copies[-1].start()
    even, odd = even * near_gain, odd * near_gain
    coef = jnp.concatenate([even * cos - odd * sin, even * sin + odd * cos], axis=1)
    value = jnp.dot(coef, table[...], precision=TOP, preferred_element_type=jnp.float32)
    near = jnp.sum(value * spread[...], axis=0, keepdims=True)
    for step, copy in enumerate(copies, 1):
        copy.wait()
        total = total + struct_in[step]
    far_coef = total * jnp.concatenate([far_gain, far_gain], axis=1)
    far = jnp.dot(far_coef, table[...], precision=TOP, preferred_element_type=jnp.float32)
    field = near + far
    potential[...] = field
    scaled[...] = weights[...] * field
    keep = pltpu.make_async_copy(scaled, scaled_all.at[me], local_sem.at[0])
    keep.start()
    copies = to_peers(lambda mask: scaled, lambda mask: scaled_all.at[me], psend, precv)
    for outs in list(results.values())[-2:]:
        for copy in outs:
            copy.wait()
    for copy in started:
        copy.wait_send()
    for copy in copies:
        copy.wait()
    keep.wait()


def hamilton_kernel(
    meta, orb, orb_flip, scaled, density8, potential8, out, density, potential,
    total, scaled_orb, block, chosen,
):
    e = pl.program_id(0)
    me = lax.axis_index("dev")
    stored = out.shape[0]
    points, width = orb.shape[1:]
    blocks = width // TB

    @pl.when(e == 0)
    def _():
        total[...] = jnp.zeros_like(total)
        for q in range(points // TB):
            density[q : q + 1, :] = density8[0:1, q * TB : (q + 1) * TB]
            potential[q : q + 1, :] = potential8[0:1, q * TB : (q + 1) * TB]

    count = jnp.int32(0)
    for r in range(blocks * blocks):
        code = meta[e, 0, r] - me * stored
        chosen[count] = r
        count = count + ((code >= 0) & (code < stored)).astype(jnp.int32)
    column = jnp.broadcast_to(scaled[0, 0:1, :], (TB, points)).T
    for j in range(blocks):
        cols = slice(j * TB, (j + 1) * TB)
        scaled_orb[:, cols] = (column * orb[0, :, cols].astype(jnp.float32)).astype(jnp.bfloat16)
    for c in range(0, blocks, 2):
        some = min(2, blocks - c)
        product = jnp.dot(
            orb_flip[0], scaled_orb[:, c * TB : (c + some) * TB],
            preferred_element_type=jnp.float32,
        )
        for t in range(some):
            block[c + t] = product[:, t * TB : (t + 1) * TB]

    def add(q, carry):
        r = chosen[q]
        i = r // blocks
        slot = meta[e, 0, r] - me * stored
        piece = block[r - i * blocks, pl.ds(pl.multiple_of(i * TB, TB), TB), :]
        total[slot] = total[slot] + piece
        return carry

    lax.fori_loop(0, count, add, 0)

    @pl.when(e == pl.num_programs(0) - 1)
    def _():
        out[...] = total[...].astype(jnp.bfloat16)


def on_device(
    n, regions, orbitals, dens_tiles, point_coords, point_weights, batch_blocks,
    tile_owner, tile_slot, batch_atoms, batch_weights, atom_grid_index,
):
    stored = dens_tiles.shape[0]
    listed = tile_slot.shape[0]
    batches, points, width = orbitals.shape
    here = batches * points
    union = math.isqrt(listed)
    wide = union * TB
    rows = -(-atom_grid_index.shape[1] // 8) * 8
    code = tile_owner[:, 0] * stored + tile_slot
    blocks = width // TB
    hit = batch_blocks[:, None, :] == jnp.arange(union, dtype=jnp.int32)[None, :, None]
    place = blocks - jnp.sum(
        jnp.where(hit, blocks - jnp.arange(blocks, dtype=jnp.int32), 0), axis=2
    )
    meta = jnp.concatenate(
        [
            jnp.pad(code, (0, TB - listed))[None],
            jnp.pad(place.reshape(-1), (0, TB - batches * union))[None],
            jnp.zeros((6, TB), jnp.int32),
        ]
    )
    f32, i32, bf16 = jnp.float32, jnp.int32, jnp.bfloat16
    S = jax.ShapeDtypeStruct
    dma = pltpu.SemaphoreType.DMA
    V = pltpu.VMEM
    density, potential, scaled_all, meta_all, union_all, flip_all = pl.pallas_call(
        functools.partial(region_kernel, n, regions),
        out_shape=(
            S((8, here), f32),
            S((8, here), f32),
            S((n, 8, here), f32),
            S((n, 8, TB), i32),
            S((n, here, wide), bf16),
            S((n, wide, here), bf16),
        ),
        in_specs=[ANY, VM, VM, VM, ANY, SM, SM, SM],
        out_specs=(VM, VM, VM, ANY, ANY, ANY),
        scratch_shapes=[
            V((KM, here), f32),
            V((2, rows, HALF), f32),
            V((rows, here), f32),
            V((rows, HALF), f32),
            V((n * stored, TB, TB), bf16),
            V((wide, wide), bf16),
            V((2, here, wide), bf16),
            V((2, wide, here), bf16),
            V((n, 8, here), f32),
            V((n, 8, here), f32),
            V((rows, KM), f32),
            V((n, rows, KM), f32),
            V((8, KM), f32),
            V((regions, 8, KM), f32),
            V((8, here), f32),
            pltpu.SMEM((n, 8, TB), i32),
            dma((batches, blocks)),
            dma((2,)),
            dma((batches, n)), dma((batches, n)),
            dma((n,)), dma((n,)), dma((n,)), dma((n,)), dma((n,)), dma((n,)),
            dma((regions,)), dma((regions,)), dma((n,)), dma((n,)), dma((n,)), dma((n,)),
            *[V((batches, blocks + 1, points, TB), bf16) for _ in range(n)],
        ],
        compiler_params=pltpu.CompilerParams(collective_id=0, has_side_effects=True),
        name="region",
    )(
        orbitals, meta, point_coords, point_weights.reshape(1, here), dens_tiles,
        batch_atoms, batch_weights, atom_grid_index,
    )
    ham_tiles, density, potential = pl.pallas_call(
        hamilton_kernel,
        grid=(n,),
        out_shape=(
            S((stored, TB, TB), bf16), S((here // TB, TB), f32), S((here // TB, TB), f32),
        ),
        in_specs=[
            SM,
            pl.BlockSpec((1, here, wide), lambda e: (e, 0, 0)),
            pl.BlockSpec((1, wide, here), lambda e: (e, 0, 0)),
            pl.BlockSpec((1, 8, here), lambda e: (e, 0, 0)),
            VM,
            VM,
        ],
        out_specs=(VM, VM, VM),
        scratch_shapes=[
            V((stored, TB, TB), f32),
            V((here, wide), bf16),
            V((union, wide, TB), f32),
            pltpu.SMEM((listed + 1,), i32),
        ],
        name="hamilton",
    )(meta_all, union_all, flip_all, scaled_all, density, potential)
    return density.reshape(-1), potential.reshape(-1), ham_tiles


def solution(mesh):
    body = functools.partial(on_device, mesh.shape["dev"], mesh.shape["grp"])
    in_specs = (
        P(("grp", "dev"), None, None),
        P(("grp", "dev"), None, None),
        P(None, ("grp", "dev")),
        P(("grp", "dev")),
        P(("grp", "dev"), None),
        P(("grp", "dev"), None),
        P(("grp", "dev")),
        P(("grp", "dev"), None),
        P(("grp", "dev"), None),
        P(None, "grp"),
    )
    out_specs = (P(("grp", "dev")), P(("grp", "dev")), P(("grp", "dev"), None, None))
    return jax.shard_map(body, mesh=mesh, in_specs=in_specs, out_specs=out_specs, check_vma=False)
```

time: 102 us -> 79.7 us (0.78)
  Pallas kernels: 96.6 us -> 76.8 us
  local copies, waits for them, and re-layouts: 3.43 us -> 0.17 us
    pallas_call x4 -> x2, Pallas kernels: 96.6 us -> 76.8 us  [the longest x1 63.5 us: on_device(): pl.pallas_call(functools.partial(region_kernel, n, regions), out_shape=(S...]
    slice x2 -> x0, local copies, waits for them, and re-layouts: 2.59 us -> none  [on_device(): return (density[0], potential[0], ham_tiles)]
where the time goes in v2:
time: 79.7 us; the launch traced here: 79.8 us
  Pallas kernels  76.8 us (96%)
  other arithmetic  2.11 us (3%)
    pallas_call x1, Pallas kernels, on_device(): pl.pallas_call(functools.partial(region_kernel, n, regions), out_shape=(S...  63.5 us
    pallas_call x1, Pallas kernels, on_device(): pl.pallas_call(hamilton_kernel, grid=(n,), out_shape=(S((stored, TB, TB),...  13.3 us

profile of v2, /device:TPU:0, one launch (start us, length us, event | category | flops | bytes accessed | tf_op | source)
XLA Modules:
  0.0 79.8 jit_solution(17257212125535402643)
XLA Ops:
  0.6 0.7 bitcast_add_fusion
  1.3 0.1 pad.12.clone
  1.4 0.8 select_reduce_fusion
  2.2 0.1 sub.12
  2.3 0.7 add_add_fusion.meta
  2.9 63.5 %region.1 = (f32[8,512]{1,0:T(8,128)}, f32[8,512]{1,0:T(8,128)}, f32[4,8,512]{2,1,0:T(8,128)}, s32[4,8,128]{2,1,0:T(8,128)}, bf16[4,512,1152]{2,1,0:T(8,128)(2,1)}, /*index=5*/bf16[4,1152,512]{2,1,0:T(8,128)(2,1)}) custom-call(bf16[2,256,1024]{2,1,0:T(8,128)(2,1)} %orb.1, s32[8,128]{1,0:T(8,128)} %add_add_fusion.meta, f32[3,512]{1,0:T(4,128)} %coords.1, ...), custom_call_target="tpu_custom_call" | custom-call | tf_op jit(solution)/shard_map/region/pallas_call | solution.py:380
  66.5 13.3 %hamilton.1 = (bf16[32,128,128]{2,1,0:T(8,128)(2,1)}, f32[4,128]{1,0:T(4,128)}, f32[4,128]{1,0:T(4,128)}) custom-call(s32[4,8,128]{2,1,0:T(8,128)} %get-tuple-element.12.meta, bf16[4,512,1152]{2,1,0:T(8,128)(2,1)} %get-tuple-element.13.orb, bf16[4,1152,512]{2,1,0:T(8,128)(2,1)} %get-tuple-element.14.orb_flip, f32[4,8,512]{2,1,0:T(8,128)} %get-tuple-element.15.scaled, ...), custom_call_target="tpu_custom_call" | custom-call | tf_op jit(solution)/shard_map/hamilton/pallas_call | solution.py:422
  (4 shorter events, 0.0 us)

commit v3 on v2

--- a/solution.py
+++ b/solution.py
@@ -13,7 +13,6 @@
 GRIDN = 64
 HALF = KM // 2
 MESH = pl.DeviceIdType.MESH
-TOP = lax.Precision.HIGHEST
 VM = pl.BlockSpec(memory_space=pltpu.VMEM)
 SM = pl.BlockSpec(memory_space=pltpu.SMEM)
 ANY = pl.BlockSpec(memory_space=pl.ANY)
@@ -29,10 +28,24 @@
     return jnp.cos(angle), jnp.sin(angle)
 
 
+def split(value):
+    high = value.astype(jnp.bfloat16)
+    return high, (value - high.astype(jnp.float32)).astype(jnp.bfloat16)
+
+
+def split_dot(value, table):
+    rows = value.shape[0]
+    high = value.astype(jnp.bfloat16)
+    rest = value - high.astype(jnp.float32)
+    both = jnp.concatenate([value, rest], axis=0).astype(jnp.bfloat16)
+    out = jnp.dot(both, table[0], preferred_element_type=jnp.float32)
+    return out[:rows] + out[rows:] + jnp.dot(high, table[1], preferred_element_type=jnp.float32)
+
+
 def region_kernel(
     n, regions, orb, meta, coords, weights, dens, atoms_s, weights_s, grid_s,
     density, potential, scaled_all, meta_all, union_all, flip_all,
-    table, phase, spread, turns, tiles, block, union, flip, part, part_in,
+    table, table_t, phase, spread, turns, tiles, block, union, flip, part, part_in,
     terms, terms_in, struct, struct_in, scaled, meta_s,
     pack_sem, local_sem, send, recv, msend, mrecv, dsend, drecv, tsend, trecv, ssend, srecv, psend, precv,
     usem, fsem, *land,
@@ -52,17 +65,6 @@
             )
             copy.start()
             packs.append(copy)
-    for ref in land:
-        for b in range(batches):
-            ref[b, held] = jnp.zeros((points, TB), jnp.bfloat16)
-
-    def clear(t, carry):
-        tiles[t] = jnp.zeros((TB, TB), jnp.bfloat16)
-        return carry
-
-    lax.fori_loop(0, n * stored, clear, 0)
-    for copy in packs:
-        copy.wait()
     barrier = pltpu.get_barrier_semaphore()
     for mask in range(1, n):
         pl.semaphore_signal(barrier, inc=1, device_id={"dev": me ^ mask}, device_id_type=MESH)
@@ -70,6 +72,17 @@
         pl.semaphore_signal(
             barrier, inc=1, device_id={"grp": lax.rem(grp + step, regions)}, device_id_type=MESH
         )
+    for ref in land:
+        for b in range(batches):
+            ref[b, held] = jnp.zeros((points, TB), jnp.bfloat16)
+
+    def clear(t, carry):
+        tiles[t] = jnp.zeros((TB, TB), jnp.bfloat16)
+        return carry
+
+    lax.fori_loop(0, n * stored, clear, 0)
+    for copy in packs:
+        copy.wait()
     pl.semaphore_wait(barrier, n + regions - 2)
 
     def remote(src, dst, ssem, rsem, **where):
@@ -119,8 +132,17 @@
         fx, fy, fz = (v.astype(jnp.float32) for v in (k & 7, (k >> 3) & 7, k >> 6))
         at = fx * coords[0:1, :] + fy * coords[1:2, :] + fz * coords[2:3, :]
         cos, sin = turn_trig(at * (1.0 / GRIDN))
-        table[pl.ds(pl.multiple_of(c * rows, rows), rows), :] = cos
-        table[pl.ds(pl.multiple_of(HALF + c * rows, rows), rows), :] = sin
+        for first, wave in ((0, cos), (HALF, sin)):
+            high, low = split(wave)
+            at = pl.ds(pl.multiple_of(first + c * rows, rows), rows)
+            table[0, at, :] = high
+            table[1, at, :] = low
+        return carry
+
+    def turn_rows(c, carry):
+        at = pl.ds(pl.multiple_of(c * TB, TB), TB)
+        table_t[0, :, at] = table[0, at, :].T
+        table_t[1, :, at] = table[1, at, :].T
         return carry
 
     def small_tables():
@@ -163,27 +185,6 @@
                 index = meta_s[e, 1, b * blocks + u]
                 union[slot, at, u * TB : (u + 1) * TB] = land[mask][b, index]
 
-        def flip_block(u, carry):
-            first = pl.multiple_of(u * TB, TB)
-            flip[slot, pl.ds(first, TB), :] = union[slot, :, pl.ds(first, TB)].T
-            return carry
-
-        lax.fori_loop(0, blocks, flip_block, 0)
-        outs = [
-            pltpu.make_async_copy(union.at[slot], union_all.at[e], usem.at[mask]),
-            pltpu.make_async_copy(flip.at[slot], flip_all.at[e], fsem.at[mask]),
-        ]
-        for copy in outs:
-            copy.start()
-        results[mask] = outs
-
-        def row(i, carry):
-            for j in range(blocks):
-                index = meta_s[e, 0, i * blocks + j]
-                block[pl.ds(pl.multiple_of(i * TB, TB), TB), j * TB : (j + 1) * TB] = tiles[index]
-            return carry
-
-        lax.fori_loop(0, blocks, row, 0)
         total = jnp.zeros((batches * points, TB), jnp.float32)
         for c in range(0, blocks, 2):
             some = min(2, blocks - c)
@@ -202,6 +203,46 @@
             copy.start()
             density_sends.append(copy)
 
+        def flip_block(u, carry):
+            first = pl.multiple_of(u * TB, TB)
+            flip[slot, pl.ds(first, TB), :] = union[slot, :, pl.ds(first, TB)].T
+            return carry
+
+        lax.fori_loop(0, blocks, flip_block, 0)
+        outs = [
+            pltpu.make_async_copy(union.at[slot], union_all.at[e], usem.at[mask]),
+            pltpu.make_async_copy(flip.at[slot], flip_all.at[e], fsem.at[mask]),
+        ]
+        for copy in outs:
+            copy.start()
+        results[mask] = outs
+
+    def assemble(mask):
+        e = me ^ mask
+
+        def row(i, carry):
+            for j in range(blocks):
+                index = meta_s[e, 0, i * blocks + j]
+                block[pl.ds(pl.multiple_of(i * TB, TB), TB), j * TB : (j + 1) * TB] = tiles[index]
+            return carry
+
+        lax.fori_loop(0, blocks, row, 0)
+
+    arrivals = []
+    counts = {}
+    order = [0]
+    for stage in range(bits):
+        for low in range(1 << stage):
+            for b in range(batches):
+                got = 1 << order_of(b)[stage]
+                for t in range(stage):
+                    if low >> t & 1:
+                        got ^= 1 << order_of(b)[t]
+                counts[got] = counts.get(got, 0) + 1
+                arrivals.append((stage, b, got, counts[got] == batches))
+                if counts[got] == batches:
+                    order.append(got)
+    order.append(None)
     small_tables()
     chunks = HALF // rows
     lax.fori_loop(0, chunks // 2, table_rows, 0)
@@ -210,27 +251,28 @@
     to_smem = pltpu.make_async_copy(meta_all, meta_s, local_sem.at[0])
     to_smem.start()
     to_smem.wait()
+    assemble(0)
     process(0)
-    arrived = {}
-    for stage in range(bits):
-        for low in range(1 << stage):
-            for b in range(batches):
-                bit = 1 << order_of(b)[stage]
-                got = bit
-                for t in range(stage):
-                    if low >> t & 1:
-                        got ^= 1 << order_of(b)[t]
-                there = landing(got, b)
-                remote(there, there, send.at[b, got], recv.at[b, got], dev=me ^ bit).wait_recv()
-                for later in range(stage + 1, bits):
-                    copy = block_copy(b, later, got)
-                    copy.start()
-                    started.append(copy)
-                arrived[got] = arrived.get(got, 0) + 1
-                if arrived[got] == batches:
-                    process(got)
-        if stage == 0:
-            lax.fori_loop(chunks // 2, chunks, table_rows, 0)
+    assemble(order[1])
+    last = 0
+    for stage, b, got, whole in arrivals:
+        if stage != last:
+            if last == 0:
+                lax.fori_loop(chunks // 2, chunks, table_rows, 0)
+                lax.fori_loop(0, KM // TB, turn_rows, 0)
+            last = stage
+        there = landing(got, b)
+        bit = 1 << order_of(b)[stage]
+        remote(there, there, send.at[b, got], recv.at[b, got], dev=me ^ bit).wait_recv()
+        for later in range(stage + 1, bits):
+            copy = block_copy(b, later, got)
+            copy.start()
+            started.append(copy)
+        if whole:
+            process(got)
+            following = order[order.index(got) + 1]
+            if following is not None:
+                assemble(following)
 
     cos, sin = phase[0], phase[1]
     fx, fy, fz = modes((1, HALF), 1)
@@ -244,10 +286,7 @@
         rho = rho + part_in[mask]
     density[...] = rho
     source = spread[...] * (weights[...] * rho[0:1, :])
-    mine = lax.dot_general(
-        source, table[...], (((1,), (1,)), ((), ())), precision=TOP,
-        preferred_element_type=jnp.float32,
-    )
+    mine = split_dot(source, table_t)
     terms[...] = mine
     copies = to_peers(lambda mask: terms, lambda mask: terms_in.at[mask], tsend, trecv)
     for mask, copy in enumerate(copies, 1):
@@ -276,13 +315,13 @@
         copies[-1].start()
     even, odd = even * near_gain, odd * near_gain
     coef = jnp.concatenate([even * cos - odd * sin, even * sin + odd * cos], axis=1)
-    value = jnp.dot(coef, table[...], precision=TOP, preferred_element_type=jnp.float32)
+    value = split_dot(coef, table)
     near = jnp.sum(value * spread[...], axis=0, keepdims=True)
     for step, copy in enumerate(copies, 1):
         copy.wait()
         total = total + struct_in[step]
     far_coef = total * jnp.concatenate([far_gain, far_gain], axis=1)
-    far = jnp.dot(far_coef, table[...], precision=TOP, preferred_element_type=jnp.float32)
+    far = split_dot(far_coef, table)
     field = near + far
     potential[...] = field
     scaled[...] = weights[...] * field
@@ -390,7 +429,8 @@
         in_specs=[ANY, VM, VM, VM, ANY, SM, SM, SM],
         out_specs=(VM, VM, VM, ANY, ANY, ANY),
         scratch_shapes=[
-            V((KM, here), f32),
+            V((2, KM, here), bf16),
+            V((2, here, KM), bf16),
             V((2, rows, HALF), f32),
             V((rows, here), f32),
             V((rows, HALF), f32),

time: 79.7 us -> 76.3 us (0.957)
  Pallas kernels: 76.8 us -> 73 us
    pallas_call x1, Pallas kernels: 63.5 us -> 59.7 us  [on_device(): pl.pallas_call(functools.partial(region_kernel, n, regions), out_shape=(S...]
where the time goes in v3:
time: 76.3 us; the launch traced here: 75.9 us
  Pallas kernels  73 us (96%)
  other arithmetic  2.11 us (3%)
    pallas_call x1, Pallas kernels, on_device(): pl.pallas_call(functools.partial(region_kernel, n, regions), out_shape=(S...  59.7 us
    pallas_call x1, Pallas kernels, on_device(): pl.pallas_call(hamilton_kernel, grid=(n,), out_shape=(S((stored, TB, TB),...  13.3 us

profile of v3, /device:TPU:0, one launch (start us, length us, event | category | flops | bytes accessed | tf_op | source)
XLA Modules:
  0.0 75.9 jit_solution(1384053174643852923)
XLA Ops:
  0.6 0.7 bitcast_add_fusion
  1.3 0.1 pad.12.clone
  1.4 0.8 %select_reduce_fusion = s32[2,9]{1,0:T(2,128)S(1)} fusion(s32[8]{0:T(128)S(1)} %iota_subtract_fusion, s32[2,8]{1,0:T(2,128)} %param.14), kind=kLoop, calls=%fused_computation | loop fusion | flops 414 | bytes 168 | tf_op jit(solution)/shard_map/reduce_sum | solution.py:405
  2.2 0.1 sub.12
  2.3 0.7 add_add_fusion.meta
  2.9 59.7 %region.1 = (f32[8,512]{1,0:T(8,128)}, f32[8,512]{1,0:T(8,128)}, f32[4,8,512]{2,1,0:T(8,128)}, s32[4,8,128]{2,1,0:T(8,128)}, bf16[4,512,1152]{2,1,0:T(8,128)(2,1)}, /*index=5*/bf16[4,1152,512]{2,1,0:T(8,128)(2,1)}) custom-call(bf16[2,256,1024]{2,1,0:T(8,128)(2,1)} %orb.1, s32[8,128]{1,0:T(8,128)} %add_add_fusion.meta, f32[3,512]{1,0:T(4,128)} %coords.1, ...), custom_call_target="tpu_custom_call" | custom-call | tf_op jit(solution)/shard_map/region/pallas_call | solution.py:419
  62.6 13.3 %hamilton.1 = (bf16[32,128,128]{2,1,0:T(8,128)(2,1)}, f32[4,128]{1,0:T(4,128)}, f32[4,128]{1,0:T(4,128)}) custom-call(s32[4,8,128]{2,1,0:T(8,128)} %get-tuple-element.12.meta, bf16[4,512,1152]{2,1,0:T(8,128)(2,1)} %get-tuple-element.13.orb, bf16[4,1152,512]{2,1,0:T(8,128)(2,1)} %get-tuple-element.14.orb_flip, f32[4,8,512]{2,1,0:T(8,128)} %get-tuple-element.15.scaled, ...), custom_call_target="tpu_custom_call" | custom-call | tf_op jit(solution)/shard_map/hamilton/pallas_call | solution.py:462
  (4 shorter events, 0.0 us)
